TPU v7x, 32 devices: a whole 2x2x4 slice. The times are simulated.
32 devices in a mesh: expert: 4 (over z), dp: 8 (over y, x, core).
Axes of the slice: x: 2, y: 2, z: 4, core: 2. Of those that a mesh axis runs over, the one named last changes fastest.
Arguments:
- row_acts: bfloat16 [4, 8192, 2048], P('expert', 'dp'), may hold values from -6 to 6
- row_grads: bfloat16 [4, 8192, 768], P('expert', 'dp'), may hold values from -6 to 6
- grad_factor: bfloat16 [4, 768, 768], P('expert', None, 'dp'), may hold values from -0.21875 to 0.21875
- value_factor: bfloat16 [4, 2048, 768], P('expert', None, 'dp'), may hold values from -0.125 to 0.125
- counts: int32 [4, 8], P('expert', 'dp'), may hold values from 128 to 1024, as said below
- row_token: int32 [4, 8192], P('expert', 'dp'), may hold values from 0 to 1023, as said below
Outputs:
- influence: float32 [8192, 24], P(('expert', 'dp'))
Inputs may be any that keep to these rules, and one draw needn't show every extreme that they name: counts[e, b] slots at the start of each block of 1024 slots are live; some block has all 1024 live. `row_token`: within one block of 1024 slots of one expert the ids are distinct, dead slots included.
All inputs are finite; a program needn't handle non-finite values.
Results may differ from a plain program's by a relative error of at most 0.0003.
Values may be sent and summed in bfloat16 or wider, within the bound.
A program may use at most 64 MiB of HBM per device.

v0:
```python
import functools

import jax
import jax.numpy as jnp
from jax import lax
from jax.experimental import pallas as pl
from jax.experimental.pallas import tpu as pltpu
from jax.sharding import PartitionSpec as P

RANK = 32
TOK_DEV = 256
LANES = 128
PACK = 16
V_PARTS = (2, 4, 4)

epsilon = 1e-06
MESH = pl.DeviceIdType.MESH
CONTRACT_LAST = (((1,), (1,)), ((), ()))


def round_up(value, unit):
    return -(-value // unit) * unit


def kernel(
    dims,
    count_ref,
    token_ref,
    acts_hbm,
    grads_hbm,
    gfac_hbm,
    vfac_hbm,
    out_ref,
    acts,
    grads,
    gfac,
    vfac,
    gproj,
    aproj,
    scores,
    onehot,
    dense,
    landed,
    far_dense,
    far_landed,
    load_sem,
    send_sem,
    recv_sem,
    zsend_sem,
    zrecv_sem,
):
    n_dp, n_exp, across, queries, real_cols = dims
    chips = n_dp // 2
    half = chips // 2
    rows, model = acts.shape
    cols = gfac.shape[2]
    me_e = lax.axis_index("expert")
    me = lax.axis_index("dp")
    core = me % 2
    other = 1 - core

    def walk(index):
        line, at = index // across, index % across
        back = line % 2
        return line * across + at + back * (across - 1 - 2 * at)

    place = walk(me // 2)

    def chip_at(step):
        return walk((place + step + chips) % chips)

    mine = chip_at(0)
    ahead = chip_at(1) * 2 + core
    behind = chip_at(-1) * 2 + core
    partner = mine * 2 + other

    pieces, start = [None], 0
    for part in V_PARTS:
        pieces.append(pl.ds(start, model // part))
        start += model // part

    def held(chip, side, piece):
        if pieces[piece] is None:
            return gfac.at[chip, side]
        return vfac.at[chip, side, :, pieces[piece]]

    def own(piece):
        if pieces[piece] is None:
            return gfac_hbm
        return vfac_hbm.at[:, pieces[piece]]

    sent = []

    def send(src, chip, side, piece, target):
        copy = pltpu.make_async_remote_copy(
            src_ref=src,
            dst_ref=held(chip, side, piece),
            send_sem=send_sem.at[len(sent)],
            recv_sem=recv_sem.at[chip, side, piece],
            device_id=(me_e, target),
            device_id_type=MESH,
        )
        copy.start()
        sent.append(copy)

    def arrived(chip, side, piece):
        pltpu.make_async_remote_copy(
            src_ref=held(chip, side, piece),
            dst_ref=held(chip, side, piece),
            send_sem=send_sem.at[0],
            recv_sem=recv_sem.at[chip, side, piece],
            device_id=(me_e, partner),
            device_id_type=MESH,
        ).wait_recv()

    loads = [
        pltpu.make_async_copy(own(j), held(mine, core, j), load_sem.at[j])
        for j in range(len(pieces))
    ]
    load_grads = pltpu.make_async_copy(grads_hbm, grads, load_sem.at[len(pieces)])
    load_acts = pltpu.make_async_copy(acts_hbm, acts, load_sem.at[len(pieces) + 1])

    barrier = pltpu.get_barrier_semaphore()
    for target in (ahead, behind, partner):
        pl.semaphore_signal(barrier, inc=1, device_id=(me_e, target), device_id_type=MESH)
    for i in range(1, n_exp):
        pl.semaphore_signal(
            barrier, inc=1, device_id=((me_e + i) % n_exp, me), device_id_type=MESH
        )
    for copy in loads:
        copy.start()
    load_grads.start()
    load_acts.start()
    pl.semaphore_wait(barrier, 3 + n_exp - 1)

    for j in range(len(pieces)):
        send(own(j), mine, core, j, ahead)
        send(own(j), mine, core, j, behind)
        send(own(j), mine, core, j, partner)

    token_ids = lax.broadcasted_iota(jnp.int32, onehot.shape, 0)
    slot_ids = lax.broadcasted_iota(jnp.int32, (1, rows), 1)
    names = jnp.where(slot_ids < count_ref[0, 0], token_ref[...], -1)
    onehot[...] = (token_ids == names).astype(jnp.float32).astype(onehot.dtype)
    load_grads.wait()
    load_acts.wait()

    def energy(ref):
        total = jnp.zeros((rows, LANES), jnp.float32)
        for i in range(ref.shape[1] // LANES):
            part = ref[:, i * LANES : (i + 1) * LANES].astype(jnp.float32)
            total = total + part * part
        return jnp.sum(total, axis=1, keepdims=True)

    lane_ids = lax.broadcasted_iota(jnp.int32, (rows, LANES), 1)
    scores[...] = jnp.where(lane_ids == queries, energy(acts) * energy(grads), 0.0)

    def project_grads(chip, buf):
        factor = gfac[chip].reshape(2 * cols, gfac.shape[3])
        gproj[buf] = lax.dot_general(
            grads[...], factor, CONTRACT_LAST, preferred_element_type=jnp.float32
        )

    def project_acts(chip, span):
        factor = vfac[chip, :, :, span].reshape(2 * cols, span.size)
        return lax.dot_general(
            acts[:, span], factor, CONTRACT_LAST, preferred_element_type=jnp.float32
        )

    def split(value):
        high = value.astype(jnp.bfloat16)
        return high, (value - high.astype(jnp.float32)).astype(jnp.bfloat16)

    def score(chip, product, first):
        local_ids = lax.broadcasted_iota(jnp.int32, (2 * cols, LANES), 0)
        query_ids = lax.broadcasted_iota(jnp.int32, (2 * cols, LANES), 1) + first
        second = (local_ids >= cols).astype(jnp.int32)
        column = (2 * chip + second) * real_cols + local_ids - second * cols
        low = query_ids * RANK
        grouping = (column >= low) & (column < low + RANK) & (query_ids < queries)
        grouping = grouping.astype(jnp.float32).astype(jnp.bfloat16)
        high, rest = split(product)
        return jnp.dot(high, grouping, preferred_element_type=jnp.float32) + jnp.dot(
            rest, grouping, preferred_element_type=jnp.float32
        )

    def hand_over(total, stage, own_sums, others):
        summed = jnp.dot(
            onehot[...],
            jnp.concatenate(split(total), axis=1),
            preferred_element_type=jnp.float32,
        )
        turned = (summed[:, :LANES] + summed[:, LANES:]).T[: own_sums.shape[1]]
        for i in range(n_exp):
            own_sums[i] = turned[:, i * TOK_DEV : (i + 1) * TOK_DEV]
        copies = []
        for i in range(1, n_exp):
            target = (me_e + i) % n_exp
            copy = pltpu.make_async_remote_copy(
                src_ref=own_sums.at[target],
                dst_ref=others.at[i - 1],
                send_sem=zsend_sem.at[stage, i - 1],
                recv_sem=zrecv_sem.at[stage, i - 1],
                device_id=(target, me),
                device_id_type=MESH,
            )
            copy.start()
            copies.append(copy)
        return copies

    def collect(copies, own_sums, others):
        result = own_sums[me_e]
        for i, copy in enumerate(copies):
            copy.wait_recv()
            result = result + others[i]
        return result

    for j in range(len(pieces)):
        loads[j].wait()
        arrived(mine, other, j)
        if j == 0:
            project_grads(mine, 0)
    aproj[0] = project_acts(mine, pl.ds(0, model))
    scores[...] += score(mine, aproj[0] * gproj[0], 0)

    def sources_of(step):
        return [chip_at(-step)] if step == half else [chip_at(-step), chip_at(step)]

    def pass_on(step, j):
        sources = sources_of(step)
        for chip in sources:
            arrived(chip, core, j)
            send(held(chip, core, j), chip, core, j, partner)
        if step < half - 1:
            send(held(sources[0], core, j), sources[0], core, j, ahead)
            send(held(sources[1], core, j), sources[1], core, j, behind)
        elif step == half - 1:
            chip = chip_at(step * (2 * core - 1))
            target = chip_at(1 - 2 * core) * 2 + core
            send(held(chip, core, j), chip, core, j, target)

    far_chip = chip_at(half)
    base = 2 * far_chip * real_cols // RANK

    def multiply(step, j):
        far_scores = None
        for buf, chip in enumerate(sources_of(step)):
            arrived(chip, other, j)
            if j == 0:
                project_grads(chip, buf)
            elif j == 1:
                aproj[buf] = project_acts(chip, pieces[j])
            elif j < len(pieces) - 1:
                aproj[buf] += project_acts(chip, pieces[j])
            else:
                product = (aproj[buf] + project_acts(chip, pieces[j])) * gproj[buf]
                if step == half:
                    far_scores = score(chip, product, base)
                else:
                    scores[...] += score(chip, product, 0)
        return far_scores

    order = [(step, j) for step in range(1, half + 1) for j in range(len(pieces))]
    done, near = 0, None
    for at, (step, j) in enumerate(order):
        pass_on(step, j)
        if step == half and j == 1:
            near = hand_over(scores[...], 0, dense, landed)
        lag = 1 if order[done][0] < half else 2
        if at - done >= lag:
            multiply(*order[done])
            done += 1
    for event in order[done:]:
        far_scores = multiply(*event)

    far = hand_over(far_scores, 1, far_dense, far_landed)
    result = collect(near, dense, landed)
    late = collect(far, far_dense, far_landed)
    row_ids = lax.broadcasted_iota(jnp.int32, result.shape, 0)
    for i in range(late.shape[0]):
        result = result + jnp.where(row_ids == base + i, late[i : i + 1], 0.0)
    energy_sum = result[queries : queries + 1]
    factor = lax.rsqrt(energy_sum / (model * grads.shape[1]) + epsilon)
    factor = factor / jnp.sqrt(jnp.float32(RANK))
    out_ref[...] = result[:queries] * factor
    for copy in near + far + sent:
        copy.wait_send()


def local(dims, row_acts, row_grads, grad_factor, value_factor, counts, row_token):
    n_dp, n_exp, across, queries, real_cols = dims
    gfac, vfac = grad_factor[0].T, value_factor[0].T
    cols = round_up(real_cols, PACK)
    if cols != real_cols:
        pad = ((0, cols - real_cols), (0, 0))
        gfac, vfac = jnp.pad(gfac, pad), jnp.pad(vfac, pad)
    rows, model = row_acts.shape[1:]
    units = row_grads.shape[2]
    chips = n_dp // 2
    depth = round_up(queries + 1, 8)
    n_pieces = 1 + len(V_PARTS)
    few = round_up((2 * real_cols - 1) // RANK + 2, 8)
    bufs = 2
    n_sends = n_pieces * (3 + sum(
        (1 if s == chips // 2 else 3 if s == chips // 2 - 1 else 4)
        for s in range(1, chips // 2 + 1)
    ))
    any_space = pl.BlockSpec(memory_space=pl.ANY)
    turned = pl.pallas_call(
        functools.partial(kernel, dims),
        name="influence_exchange",
        out_shape=jax.ShapeDtypeStruct((queries, TOK_DEV), jnp.float32),
        in_specs=[
            pl.BlockSpec(memory_space=pltpu.SMEM),
            pl.BlockSpec(memory_space=pltpu.VMEM),
            any_space,
            any_space,
            any_space,
            any_space,
        ],
        out_specs=pl.BlockSpec(memory_space=pltpu.VMEM),
        scratch_shapes=[
            pltpu.VMEM((rows, model), jnp.bfloat16),
            pltpu.VMEM((rows, units), jnp.bfloat16),
            pltpu.VMEM((chips, 2, cols, units), jnp.bfloat16),
            pltpu.VMEM((chips, 2, cols, model), jnp.bfloat16),
            pltpu.VMEM((bufs, rows, 2 * cols), jnp.float32),
            pltpu.VMEM((bufs, rows, 2 * cols), jnp.float32),
            pltpu.VMEM((rows, LANES), jnp.float32),
            pltpu.VMEM((n_exp * TOK_DEV, rows), jnp.bfloat16),
            pltpu.VMEM((n_exp, depth, TOK_DEV), jnp.float32),
            pltpu.VMEM((n_exp - 1, depth, TOK_DEV), jnp.float32),
            pltpu.VMEM((n_exp, few, TOK_DEV), jnp.float32),
            pltpu.VMEM((n_exp - 1, few, TOK_DEV), jnp.float32),
            pltpu.SemaphoreType.DMA((n_pieces + 2,)),
            pltpu.SemaphoreType.DMA((n_sends,)),
            pltpu.SemaphoreType.DMA((chips, 2, n_pieces)),
            pltpu.SemaphoreType.DMA((2, n_exp - 1)),
            pltpu.SemaphoreType.DMA((2, n_exp - 1)),
        ],
        compiler_params=pltpu.CompilerParams(
            collective_id=0, has_side_effects=True, vmem_limit_bytes=60 * 1024 * 1024
        ),
    )(counts, row_token, row_acts[0], row_grads[0], gfac, vfac)
    return turned.T


def solution(mesh):
    n_exp, n_dp = mesh.shape["expert"], mesh.shape["dp"]
    across = len({d.coords[0] for d in mesh.devices.flat})

    def whole(row_acts, row_grads, grad_factor, value_factor, counts, row_token):
        all_cols = grad_factor.shape[2]
        dims = (n_dp, n_exp, across, all_cols // RANK, all_cols // n_dp)
        return jax.shard_map(
            functools.partial(local, dims),
            mesh=mesh,
            in_specs=(
                P("expert", "dp", None),
                P("expert", "dp", None),
                P("expert", None, "dp"),
                P("expert", None, "dp"),
                P("expert", "dp"),
                P("expert", "dp"),
            ),
            out_specs=P(("expert", "dp"), None),
            check_vma=False,
        )(row_acts, row_grads, grad_factor, value_factor, counts, row_token)

    return whole
```

profile of v0, /device:TPU:0, one launch (start us, length us, event | category | flops | bytes accessed | tf_op | source)
XLA Modules:
  0.0 37.6 jit_solution(9472825934804465147)
XLA Ops:
  0.7 35.6 %influence_exchange.1 = f32[24,256]{1,0:T(8,128)} custom-call(s32[1,1]{1,0:T(1,128)S(6)} %copy.8.count_ref, s32[1,1024]{1,0:T(1,128)} %token_ref.1, bf16[1024,2048]{1,0:T(8,128)(2,1)} %bitcast.9, bf16[1024,768]{1,0:T(8,128)(2,1)} %bitcast.10, bf16[96,768]{1,0:T(8,128)(2,1)} %bitcast.12, bf16[96,2048]{1,0:T(8,128)(2,1)} %bitcast.11), custom_call_target="tpu_custom_call" | custom-call | tf_op jit(solution)/shard_map/influence_exchange/pallas_call | solution.py:309
  36.2 1.3 %copy.9 = f32[256,24]{0,1:T(8,128)} copy(f32[256,24]{0,1:T(8,128)} %bitcast.13) | data formatting | bytes 49152
where the time goes:
time: 37.8 us; the launch traced here: 37.6 us
  Pallas kernels  35.6 us (94%)
  local copies, waits for them, and re-layouts  1.35 us (4%)
  between operations  0.66 us (2%)
    pallas_call x1, Pallas kernels, local(): pl.pallas_call(functools.partial(kernel, dims), name='influence_exchange'...  35.6 us
    unnamed x1, local copies, waits for them, and re-layouts  1.35 us

commit v1 on v0

v1 whole, which is shorter than its diff:
```python
import functools

import jax
import jax.numpy as jnp
from jax import lax
from jax.experimental import pallas as pl
from jax.experimental.pallas import tpu as pltpu
from jax.sharding import PartitionSpec as P

RANK = 32
TOK_DEV = 256
LANES = 128
PACK = 16
V_PARTS = (2, 4, 8, 8)

epsilon = 1e-06
MESH = pl.DeviceIdType.MESH
CONTRACT_LAST = (((1,), (1,)), ((), ()))


def round_up(value, unit):
    return -(-value // unit) * unit


def kernel(
    dims,
    count_ref,
    token_hbm,
    acts_hbm,
    grads_hbm,
    gfac_hbm,
    vfac_hbm,
    out_ref,
    tokens,
    acts,
    grads,
    gfac,
    vfac,
    gproj,
    aproj,
    scores,
    far_scores,
    onehot,
    dense,
    landed,
    far_dense,
    far_landed,
    load_sem,
    send_sem,
    recv_sem,
    zsend_sem,
    zrecv_sem,
):
    n_dp, n_exp, across, queries, real_cols, granule = dims
    chips = n_dp // 2
    half = chips // 2
    rows, model = acts.shape
    cols = gfac.shape[2]
    me_e = lax.axis_index("expert")
    me = lax.axis_index("dp")
    core = me % 2
    other = 1 - core

    def walk(index):
        line, at = index // across, index % across
        back = line % 2
        return line * across + at + back * (across - 1 - 2 * at)

    place = walk(me // 2)

    def chip_at(step):
        return walk((place + step + chips) % chips)

    mine = chip_at(0)
    ahead = chip_at(1) * 2 + core
    behind = chip_at(-1) * 2 + core
    partner = mine * 2 + other

    pieces, start = [None], 0
    for part in V_PARTS:
        pieces.append(pl.ds(start, model // part))
        start += model // part
    last_piece = len(pieces) - 1

    def held(chip, side, piece):
        if pieces[piece] is None:
            return gfac.at[chip, side]
        return vfac.at[chip, side, :, pieces[piece]]

    def own(piece):
        if pieces[piece] is None:
            return gfac_hbm
        return vfac_hbm.at[:, pieces[piece]]

    sent = []

    def send(src, chip, side, piece, target):
        copy = pltpu.make_async_remote_copy(
            src_ref=src,
            dst_ref=held(chip, side, piece),
            send_sem=send_sem.at[len(sent)],
            recv_sem=recv_sem.at[chip, side, piece],
            device_id=(me_e, target),
            device_id_type=MESH,
        )
        copy.start()
        sent.append(copy)

    def arrived(chip, side, piece):
        pltpu.make_async_remote_copy(
            src_ref=held(chip, side, piece),
            dst_ref=held(chip, side, piece),
            send_sem=send_sem.at[0],
            recv_sem=recv_sem.at[chip, side, piece],
            device_id=(me_e, partner),
            device_id_type=MESH,
        ).wait_recv()

    barrier = pltpu.get_barrier_semaphore()
    for target in (ahead, behind, partner):
        pl.semaphore_signal(barrier, inc=1, device_id=(me_e, target), device_id_type=MESH)
    for i in range(1, n_exp):
        pl.semaphore_signal(
            barrier, inc=1, device_id=((me_e + i) % n_exp, me), device_id_type=MESH
        )

    n_pieces = len(pieces)
    load_tokens = pltpu.make_async_copy(token_hbm, tokens, load_sem.at[n_pieces + 2])
    load_tokens.start()
    loads = [
        pltpu.make_async_copy(own(j), held(mine, core, j), load_sem.at[j])
        for j in range(n_pieces)
    ]
    load_grads = pltpu.make_async_copy(grads_hbm, grads, load_sem.at[n_pieces])
    load_acts = pltpu.make_async_copy(acts_hbm, acts, load_sem.at[n_pieces + 1])
    for copy in loads:
        copy.start()
    load_grads.start()
    load_acts.start()
    with jax.named_scope("barrier"):
        pl.semaphore_wait(barrier, 3 + n_exp - 1)

    for j in range(n_pieces):
        send(own(j), mine, core, j, ahead)
        send(own(j), mine, core, j, behind)
        send(own(j), mine, core, j, partner)

    with jax.named_scope("onehot"):
        load_tokens.wait()
        slot_ids = lax.broadcasted_iota(jnp.int32, (1, rows), 1)
        names = jnp.where(slot_ids < count_ref[0, 0], tokens[...], -1)
        names = jnp.broadcast_to(names, (LANES, rows)).T
        lane_ids = lax.broadcasted_iota(jnp.int32, (rows, LANES), 1)
        for i in range(n_exp * TOK_DEV // LANES):
            hit = (names == lane_ids + i * LANES).astype(jnp.float32)
            onehot[:, i * LANES : (i + 1) * LANES] = hit.astype(onehot.dtype)

    with jax.named_scope("loadwait"):
        load_grads.wait()
        load_acts.wait()

    def energy(ref):
        total = jnp.zeros((rows, LANES), jnp.float32)
        for i in range(ref.shape[1] // LANES):
            part = ref[:, i * LANES : (i + 1) * LANES].astype(jnp.float32)
            total = total + part * part
        return jnp.sum(total.T, axis=0, keepdims=True)

    with jax.named_scope("energy"):
        scores[...] = jnp.zeros_like(scores)
        far_scores[...] = jnp.zeros_like(far_scores)
        scores[queries : queries + 1] = energy(acts) * energy(grads)

    def project(factors, ref, span):
        factor = [f.reshape(2 * cols, f.shape[-1]) for f in factors]
        factor = jnp.concatenate(factor, axis=0) if len(factor) > 1 else factor[0]
        return lax.dot_general(
            factor, ref[:, span], CONTRACT_LAST, preferred_element_type=jnp.float32
        ).reshape(len(factors), 2, cols, rows)

    def project_grads(sources):
        gproj[: len(sources)] = project(
            [gfac[chip] for chip in sources], grads, pl.ds(0, grads.shape[1])
        )

    def project_acts(sources, span):
        return project([vfac[chip, :, :, span] for chip in sources], acts, span)

    def score(target, first, chip, side, product):
        for i in range(real_cols // granule):
            query = ((2 * chip + side) * real_cols + i * granule) // RANK - first
            part = product[i * granule : (i + 1) * granule]
            target[pl.ds(query, 1)] += jnp.sum(part, axis=0, keepdims=True)

    def owner_at(k):
        low = k + (k >= me_e).astype(jnp.int32)
        high = n_exp - 1 - k
        high = high - (high <= me_e).astype(jnp.int32)
        return jnp.where(2 * me_e < n_exp, high, low)

    def of_owner(owner):
        return pl.ds(pl.multiple_of(owner * TOK_DEV, TOK_DEV), TOK_DEV)

    def hand_over(total, stage, own_sums, others):
        depth = total.shape[0]
        high = total.astype(jnp.bfloat16).astype(jnp.float32)
        both = jnp.concatenate([high, total - high], axis=0).astype(jnp.bfloat16)

        def tokens_of(owner):
            sums = jnp.dot(
                both, onehot[:, of_owner(owner)], preferred_element_type=jnp.float32
            )
            own_sums[owner] = sums[:depth] + sums[depth:]

        copies = []
        for k in range(n_exp - 1):
            owner = owner_at(k)
            tokens_of(owner)
            copy = pltpu.make_async_remote_copy(
                src_ref=own_sums.at[owner],
                dst_ref=others.at[me_e],
                send_sem=zsend_sem.at[stage, k],
                recv_sem=zrecv_sem.at[stage, me_e],
                device_id=(owner, me),
                device_id_type=MESH,
            )
            copy.start()
            copies.append(copy)
        tokens_of(me_e)
        return copies

    def collect(stage, own_sums, others):
        result = own_sums[me_e]
        for k in reversed(range(n_exp - 1)):
            source = owner_at(k)
            pltpu.make_async_remote_copy(
                src_ref=own_sums.at[source],
                dst_ref=others.at[source],
                send_sem=zsend_sem.at[stage, k],
                recv_sem=zrecv_sem.at[stage, source],
                device_id=(source, me),
                device_id_type=MESH,
            ).wait_recv()
            result = result + others[source]
        return result

    with jax.named_scope("mine"):
        for j in range(n_pieces):
            loads[j].wait()
            arrived(mine, other, j)
            if j == 0:
                project_grads([mine])
        product = project_acts([mine], pl.ds(0, model))[0] * gproj[0]
        for side in range(2):
            score(scores, 0, mine, side, product[side])

    def sources_of(step):
        return [chip_at(-step)] if step == half else [chip_at(-step), chip_at(step)]

    def pass_on(step, j):
        sources = sources_of(step)
        for chip in sources:
            arrived(chip, core, j)
            send(held(chip, core, j), chip, core, j, partner)
        if step < half - 1:
            send(held(sources[0], core, j), sources[0], core, j, ahead)
            send(held(sources[1], core, j), sources[1], core, j, behind)
        elif step == half - 1:
            chip = chip_at(step * (2 * core - 1))
            target = chip_at(1 - 2 * core) * 2 + core
            send(held(chip, core, j), chip, core, j, target)

    far_chip = chip_at(half)
    base = 2 * far_chip * real_cols // RANK

    def multiply(step, j):
        sources = sources_of(step)
        for chip in sources:
            arrived(chip, other, j)
        count = len(sources)
        if j == 0:
            project_grads(sources)
        elif j == 1:
            aproj[:count] = project_acts(sources, pieces[j])
        elif j < last_piece:
            aproj[:count] += project_acts(sources, pieces[j])
        else:
            product = (aproj[:count] + project_acts(sources, pieces[j])) * gproj[:count]
            for buf, chip in enumerate(sources):
                for side in range(2):
                    if step == half:
                        score(far_scores, base, chip, side, product[buf, side])
                    else:
                        score(scores, 0, chip, side, product[buf, side])

    order = [(step, j) for step in range(1, half + 1) for j in range(n_pieces)]
    near = None
    for at, event in enumerate(order):
        with jax.named_scope(f"pass{event[0]}{event[1]}"):
            pass_on(*event)
        if at:
            with jax.named_scope(f"mul{order[at - 1][0]}{order[at - 1][1]}"):
                multiply(*order[at - 1])
        if event == (half, 0):
            with jax.named_scope("near"):
                near = hand_over(scores[...], 0, dense, landed)
    with jax.named_scope("mullast"):
        multiply(*order[-1])

    with jax.named_scope("far"):
        far = hand_over(far_scores[...], 1, far_dense, far_landed)
    with jax.named_scope("colnear"):
        result = collect(0, dense, landed)
        factor = lax.rsqrt(
            result[queries : queries + 1] / (model * grads.shape[1]) + epsilon
        )
        factor = factor / jnp.sqrt(jnp.float32(RANK))
    with jax.named_scope("colfar"):
        late = collect(1, far_dense, far_landed)
    row_ids = lax.broadcasted_iota(jnp.int32, result.shape, 0)
    for i in range(late.shape[0]):
        result = result + jnp.where(row_ids == base + i, late[i : i + 1], 0.0)
    out_ref[...] = result[:queries] * factor
    with jax.named_scope("sends"):
        for copy in near + far + sent:
            copy.wait_send()


def local(dims, row_acts, row_grads, grad_factor, value_factor, counts, row_token):
    n_dp, n_exp, across, queries, real_cols, granule = dims
    gfac, vfac = grad_factor[0].T, value_factor[0].T
    cols = round_up(real_cols, PACK)
    if cols != real_cols:
        pad = ((0, cols - real_cols), (0, 0))
        gfac, vfac = jnp.pad(gfac, pad), jnp.pad(vfac, pad)
    rows, model = row_acts.shape[1:]
    units = row_grads.shape[2]
    chips = n_dp // 2
    depth = round_up(queries + 1, 8)
    n_pieces = 1 + len(V_PARTS)
    few = round_up((2 * real_cols - 1) // RANK + 2, 8)
    bufs = 2
    n_sends = n_pieces * (3 + sum(
        (1 if s == chips // 2 else 3 if s == chips // 2 - 1 else 4)
        for s in range(1, chips // 2 + 1)
    ))
    any_space = pl.BlockSpec(memory_space=pl.ANY)
    turned = pl.pallas_call(
        functools.partial(kernel, dims),
        name="influence_exchange",
        out_shape=pltpu.VMEM((queries, TOK_DEV), jnp.float32),
        in_specs=[pl.BlockSpec(memory_space=pltpu.SMEM)] + [any_space] * 5,
        out_specs=pl.BlockSpec(memory_space=pltpu.VMEM),
        scratch_shapes=[
            pltpu.VMEM((1, rows), jnp.int32),
            pltpu.VMEM((rows, model), jnp.bfloat16),
            pltpu.VMEM((rows, units), jnp.bfloat16),
            pltpu.VMEM((chips, 2, cols, units), jnp.bfloat16),
            pltpu.VMEM((chips, 2, cols, model), jnp.bfloat16),
            pltpu.VMEM((bufs, 2, cols, rows), jnp.float32),
            pltpu.VMEM((bufs, 2, cols, rows), jnp.float32),
            pltpu.VMEM((depth, rows), jnp.float32),
            pltpu.VMEM((few, rows), jnp.float32),
            pltpu.VMEM((rows, n_exp * TOK_DEV), jnp.bfloat16),
            pltpu.VMEM((n_exp, depth, TOK_DEV), jnp.float32),
            pltpu.VMEM((n_exp, depth, TOK_DEV), jnp.float32),
            pltpu.VMEM((n_exp, few, TOK_DEV), jnp.float32),
            pltpu.VMEM((n_exp, few, TOK_DEV), jnp.float32),
            pltpu.SemaphoreType.DMA((n_pieces + 3,)),
            pltpu.SemaphoreType.DMA((n_sends,)),
            pltpu.SemaphoreType.DMA((chips, 2, n_pieces)),
            pltpu.SemaphoreType.DMA((2, n_exp - 1)),
            pltpu.SemaphoreType.DMA((2, n_exp)),
        ],
        compiler_params=pltpu.CompilerParams(
            collective_id=0, has_side_effects=True, vmem_limit_bytes=60 * 1024 * 1024
        ),
    )(counts, row_token, row_acts[0], row_grads[0], gfac, vfac)
    return turned.T


def solution(mesh):
    n_exp, n_dp = mesh.shape["expert"], mesh.shape["dp"]
    across = len({d.coords[0] for d in mesh.devices.flat})

    def whole(row_acts, row_grads, grad_factor, value_factor, counts, row_token):
        all_cols = grad_factor.shape[2]
        real_cols = all_cols // n_dp
        granule = real_cols if RANK % real_cols == 0 else RANK
        while real_cols % granule:
            granule //= 2
        dims = (n_dp, n_exp, across, all_cols // RANK, real_cols, granule)
        return jax.shard_map(
            functools.partial(local, dims),
            mesh=mesh,
            in_specs=(
                P("expert", "dp", None),
                P("expert", "dp", None),
                P("expert", None, "dp"),
                P("expert", None, "dp"),
                P("expert", "dp"),
                P("expert", "dp"),
            ),
            out_specs=P(("expert", "dp"), None),
            check_vma=False,
        )(row_acts, row_grads, grad_factor, value_factor, counts, row_token)

    return whole
```

time: 37.8 us -> 32.2 us (0.85)
  Pallas kernels: 35.6 us -> 30.7 us
  local copies, waits for them, and re-layouts: 1.35 us -> 0.61 us
    pallas_call x1, Pallas kernels: 35.6 us -> 30.7 us  [local(): pl.pallas_call(functools.partial(kernel, dims), name='influence_exchange'...]
    unnamed x1, local copies, waits for them, and re-layouts: 1.35 us -> 0.61 us
where the time goes in v1:
time: 32.2 us; the launch traced here: 32 us
  Pallas kernels  30.7 us (95%)
  between operations  0.66 us (2%)
  local copies, waits for them, and re-layouts  0.61 us (2%)
    pallas_call x1, Pallas kernels, local(): pl.pallas_call(functools.partial(kernel, dims), name='influence_exchange'...  30.7 us

profile of v1, /device:TPU:0, one launch (start us, length us, event | category | flops | bytes accessed | tf_op | source)
XLA Modules:
  0.0 32.0 jit_solution(10808782869180874522)
XLA Ops:
  0.7 30.7 %influence_exchange.1 = f32[24,256]{1,0:T(8,128)S(1)} custom-call(s32[1,1]{1,0:T(1,128)S(6)} %copy.9.count_ref, s32[1,1024]{1,0:T(1,128)} %token_hbm.1, bf16[1024,2048]{1,0:T(8,128)(2,1)} %bitcast.10, bf16[1024,768]{1,0:T(8,128)(2,1)} %bitcast.11, bf16[96,768]{1,0:T(8,128)(2,1)} %bitcast.13, bf16[96,2048]{1,0:T(8,128)(2,1)} %bitcast.12), custom_call_target="tpu_custom_call" | custom-call | tf_op jit(solution)/shard_map/influence_exchange/pallas_call | solution.py:348
  31.4 0.6 %copy.8 = f32[256,24]{0,1:T(8,128)} copy(f32[256,24]{0,1:T(8,128)S(1)} %bitcast.9) | data formatting | bytes 49152

commit v2 on v1

v2 whole, which is shorter than its diff:
```python
import functools

import jax
import jax.numpy as jnp
from jax import lax
from jax.experimental import pallas as pl
from jax.experimental.pallas import tpu as pltpu
from jax.sharding import PartitionSpec as P

RANK = 32
TOK_DEV = 256
LANES = 128
PACK = 16
V_PARTS = (2, 4, 8, 8)
CHUNK = 256
CHUNKS_BEFORE_RELAY = 8

epsilon = 1e-06
MESH = pl.DeviceIdType.MESH
CONTRACT_LAST = (((1,), (1,)), ((), ()))


def round_up(value, unit):
    return -(-value // unit) * unit


def kernel(
    dims,
    count_ref,
    token_hbm,
    acts_hbm,
    grads_hbm,
    gfac_hbm,
    vfac_hbm,
    out_ref,
    tokens,
    rows,
    by_token,
    fac,
    gproj,
    aproj,
    scores,
    onehot,
    energies,
    landed,
    far_dense,
    far_landed,
    load_sem,
    send_sem,
    own_sem,
    direct_sem,
    relay_sem,
    zsend_sem,
    zrecv_sem,
):
    n_dp, n_exp, across, queries, real_cols, granule, units = dims
    chips = n_dp // 2
    half = chips // 2
    slots, width = rows.shape
    model = width - units
    n_tok = by_token.shape[0]
    cols = fac.shape[1]
    me_e = lax.axis_index("expert")
    me = lax.axis_index("dp")
    core = me % 2
    other = 1 - core

    def walk(index):
        line, at = index // across, index % across
        back = line % 2
        return line * across + at + back * (across - 1 - 2 * at)

    place = walk(me // 2)

    def chip_at(step):
        return walk((place + step + chips) % chips)

    mine = chip_at(0)
    ahead = chip_at(1) * 2 + core
    behind = chip_at(-1) * 2 + core
    partner = mine * 2 + other

    pieces, start = [pl.ds(0, units)], units
    for part in V_PARTS:
        pieces.append(pl.ds(start, model // part))
        start += model // part
    n_pieces = len(pieces)
    last_piece = n_pieces - 1

    def own(j):
        if j == 0:
            return gfac_hbm
        return vfac_hbm.at[:, pl.ds(pieces[j].start - units, pieces[j].size)]

    sent = []

    def send(src, dst, sem, target):
        copy = pltpu.make_async_remote_copy(
            src_ref=src,
            dst_ref=dst,
            send_sem=send_sem.at[0],
            recv_sem=sem,
            device_id=(me_e, target),
            device_id_type=MESH,
        )
        copy.start()
        sent.append(src.shape[0] * src.shape[1])

    def wait_for(ref, sem):
        pltpu.make_async_remote_copy(
            src_ref=ref,
            dst_ref=ref,
            send_sem=send_sem.at[0],
            recv_sem=sem,
            device_id=(me_e, partner),
            device_id_type=MESH,
        ).wait_recv()

    barrier = pltpu.get_barrier_semaphore()
    for target in (ahead, behind, partner):
        pl.semaphore_signal(barrier, inc=1, device_id=(me_e, target), device_id_type=MESH)
    for i in range(1, n_exp):
        pl.semaphore_signal(
            barrier, inc=1, device_id=((me_e + i) % n_exp, me), device_id_type=MESH
        )

    g_span, v_span = pl.ds(0, units), pl.ds(units, model)
    own_slot = mine * 2 + core
    load_tokens = pltpu.make_async_copy(token_hbm, tokens, load_sem.at[0])
    load_tokens.start()
    pltpu.make_async_copy(grads_hbm, rows.at[:, g_span], load_sem.at[1]).start()
    pltpu.make_async_copy(acts_hbm, rows.at[:, v_span], load_sem.at[1]).start()
    pltpu.make_async_copy(gfac_hbm, fac.at[own_slot, :, g_span], load_sem.at[2]).start()
    pltpu.make_async_copy(vfac_hbm, fac.at[own_slot, :, v_span], load_sem.at[2]).start()
    with jax.named_scope("barrier"):
        pl.semaphore_wait(barrier, 3 + n_exp - 1)

    for j in range(n_pieces):
        for target in (ahead, behind):
            send(own(j), fac.at[own_slot, :, pieces[j]], direct_sem.at[0, j], target)
    send(gfac_hbm, fac.at[own_slot, :, g_span], own_sem.at[0], partner)
    send(vfac_hbm, fac.at[own_slot, :, v_span], own_sem.at[0], partner)

    with jax.named_scope("onehot"):
        load_tokens.wait()
        slot_ids = lax.broadcasted_iota(jnp.int32, (1, slots), 1)
        names = jnp.where(slot_ids < count_ref[0, 0], tokens[...], -1)
        token_ids = lax.broadcasted_iota(jnp.int32, onehot.shape, 0)
        onehot[...] = (token_ids == names).astype(jnp.float32).astype(onehot.dtype)
        scores[...] = jnp.zeros_like(scores)
        far_dense[...] = jnp.zeros_like(far_dense)
        energies[...] = jnp.zeros_like(energies)

    with jax.named_scope("loadwait"):
        pltpu.make_async_copy(rows, rows, load_sem.at[1]).wait()

    def order_rows(first, size):
        part = jnp.dot(
            onehot[...], rows[:, first : first + size], preferred_element_type=jnp.float32
        )
        by_token[:, first : first + size] = part.astype(by_token.dtype)
        kind = int(first >= units)
        squares = part * part
        for i in range(size // LANES):
            energies[kind] += squares[:, i * LANES : (i + 1) * LANES]

    chunks = [(i, CHUNK) for i in range(0, width, CHUNK)]

    def project(factor, ref, span):
        return lax.dot_general(
            factor, ref[:, span], CONTRACT_LAST, preferred_element_type=jnp.float32
        )

    def project_pair(sources, span):
        factor = [fac[pl.ds(2 * chip, 2), :, span] for chip in sources]
        factor = jnp.concatenate([f.reshape(2 * cols, span.size) for f in factor], axis=0)
        return project(factor, by_token, span).reshape(len(sources), 2, cols, n_tok)

    def group_sums(chip, side, product):
        for i in range(real_cols // granule):
            query = ((2 * chip + side) * real_cols + i * granule) // RANK
            part = product[i * granule : (i + 1) * granule]
            yield query, jnp.sum(part, axis=0, keepdims=True)

    def owner_at(k):
        low = k + (k >= me_e).astype(jnp.int32)
        high = n_exp - 1 - k
        high = high - (high <= me_e).astype(jnp.int32)
        return jnp.where(2 * me_e < n_exp, high, low)

    def of_owner(owner):
        return pl.ds(pl.multiple_of(owner * TOK_DEV, TOK_DEV), TOK_DEV)

    def hand_over(stage, src, dst, owner):
        pltpu.make_async_remote_copy(
            src_ref=src,
            dst_ref=dst,
            send_sem=zsend_sem.at[stage],
            recv_sem=zrecv_sem.at[stage],
            device_id=(owner, me),
            device_id_type=MESH,
        ).start()

    def handed(stage, ref):
        all_of = ref.at[pl.ds(0, n_exp - 1)]
        return pltpu.make_async_remote_copy(
            src_ref=all_of,
            dst_ref=all_of,
            send_sem=zsend_sem.at[stage],
            recv_sem=zrecv_sem.at[stage],
            device_id=((me_e + 1) % n_exp, me),
            device_id_type=MESH,
        )

    def sources_of(step):
        return [chip_at(-step)] if step == half else [chip_at(-step), chip_at(step)]

    def pass_on(step, j):
        sources = sources_of(step)
        count = len(sources)
        span = pieces[j]
        wait_for(fac.at[pl.ds(0, count), :, span], direct_sem.at[step - 1, j])

        def relay(chip, sem, target):
            part = fac.at[2 * chip + core, :, span]
            send(part, part, sem, target)

        if step < half - 1:
            relay(sources[0], direct_sem.at[step, j], ahead)
            relay(sources[1], direct_sem.at[step, j], behind)
        elif step == half - 1:
            chip = chip_at(step * (2 * core - 1))
            target = chip_at(1 - 2 * core) * 2 + core
            relay(chip, direct_sem.at[step, j], target)
        for chip in sources:
            relay(chip, relay_sem.at[step - 1, j], partner)

    def relayed(step, j):
        count = len(sources_of(step))
        wait_for(fac.at[pl.ds(0, count), :, pieces[j]], relay_sem.at[step - 1, j])

    far_chip = chip_at(half)
    base = 2 * far_chip * real_cols // RANK

    def multiply(step, j):
        sources = sources_of(step)
        count = len(sources)
        relayed(step, j)
        value = project_pair(sources, pieces[j])
        if j == 0:
            gproj[:count] = value
        elif j == 1:
            aproj[:count] = value
        elif j < last_piece:
            aproj[:count] += value
        else:
            product = (aproj[:count] + value) * gproj[:count]
            for buf, chip in enumerate(sources):
                for side in range(2):
                    for query, total in group_sums(chip, side, product[buf, side]):
                        scores[pl.ds(query, 1)] += total

    with jax.named_scope("perm"):
        for chunk in chunks[:CHUNKS_BEFORE_RELAY]:
            order_rows(*chunk)
    with jax.named_scope("pass10"):
        pass_on(1, 0)
    with jax.named_scope("perm2"):
        for chunk in chunks[CHUNKS_BEFORE_RELAY:]:
            order_rows(*chunk)
    with jax.named_scope("energy"):
        totals = [
            jnp.sum(energies[kind].T, axis=0, keepdims=True) for kind in range(2)
        ]
        scores[queries : queries + 1] = totals[0] * totals[1]

    with jax.named_scope("mine"):
        own_shard = fac.at[own_slot]
        pltpu.make_async_copy(own_shard, own_shard, load_sem.at[2]).wait()
        wait_for(own_shard, own_sem.at[0])
        product = project_pair([mine], v_span)[0] * project_pair([mine], g_span)[0]
        for side in range(2):
            for query, total in group_sums(mine, side, product[side]):
                scores[pl.ds(query, 1)] += total

    order = [(step, j) for step in range(1, half + 1) for j in range(n_pieces)]
    for at, event in enumerate(order):
        if not at:
            continue
        with jax.named_scope(f"pass{event[0]}{event[1]}"):
            pass_on(*event)
        with jax.named_scope(f"mul{order[at - 1][0]}{order[at - 1][1]}"):
            multiply(*order[at - 1])
        if event == (half, 0):
            with jax.named_scope("near"):
                for k in range(n_exp - 1):
                    owner = owner_at(k)
                    hand_over(0, scores.at[:, of_owner(owner)], landed.at[me_e], owner)

    def far_sums(side, owner, product):
        for query, total in group_sums(far_chip, side, product):
            far_dense[owner, pl.ds(query - base, 1)] += total

    span = pieces[last_piece]
    with jax.named_scope("ownhalf"):
        value = project(fac[2 * far_chip + core, :, span], by_token, span)
        product = (aproj[0, core] + value) * gproj[0, core]
        for owner in range(n_exp):
            far_sums(core, owner, product[:, owner * TOK_DEV : (owner + 1) * TOK_DEV])
    with jax.named_scope("lastrelay"):
        relayed(half, last_piece)
    with jax.named_scope("far"):
        for k in range(n_exp):
            owner = owner_at(k) if k < n_exp - 1 else me_e
            tok = of_owner(owner)
            value = lax.dot_general(
                fac[2 * far_chip + other, :, span],
                by_token[tok, span],
                CONTRACT_LAST,
                preferred_element_type=jnp.float32,
            )
            far_sums(other, owner, (aproj[0, other, :, tok] + value) * gproj[0, other, :, tok])
            if k < n_exp - 1:
                hand_over(1, far_dense.at[owner], far_landed.at[me_e], owner)

    near_wait, far_wait = handed(0, landed), handed(1, far_landed)
    with jax.named_scope("colnear"):
        result = scores[:, of_owner(me_e)]
        near_wait.wait_recv()
        for k in range(n_exp - 1):
            result = result + landed[owner_at(k)]
        factor = lax.rsqrt(result[queries : queries + 1] / (model * units) + epsilon)
        factor = factor / jnp.sqrt(jnp.float32(RANK))
        late = far_dense[me_e]
    with jax.named_scope("colfar"):
        far_wait.wait_recv()
    for k in range(n_exp - 1):
        late = late + far_landed[owner_at(k)]
    row_ids = lax.broadcasted_iota(jnp.int32, result.shape, 0)
    for i in range(late.shape[0]):
        result = result + jnp.where(row_ids == base + i, late[i : i + 1], 0.0)
    out_ref[...] = result[:queries] * factor
    with jax.named_scope("sends"):
        near_wait.wait_send()
        far_wait.wait_send()
        all_sent = fac.at[pl.ds(0, sum(sent) // (cols * width))]
        pltpu.make_async_remote_copy(
            src_ref=all_sent,
            dst_ref=all_sent,
            send_sem=send_sem.at[0],
            recv_sem=own_sem.at[0],
            device_id=(me_e, partner),
            device_id_type=MESH,
        ).wait_send()


def local(dims, row_acts, row_grads, grad_factor, value_factor, counts, row_token):
    n_dp, n_exp, across, queries, real_cols, granule = dims
    gfac, vfac = grad_factor[0].T, value_factor[0].T
    cols = round_up(real_cols, PACK)
    if cols != real_cols:
        pad = ((0, cols - real_cols), (0, 0))
        gfac, vfac = jnp.pad(gfac, pad), jnp.pad(vfac, pad)
    slots, model = row_acts.shape[1:]
    units = row_grads.shape[2]
    width = units + model
    chips = n_dp // 2
    steps = chips // 2
    depth = round_up(queries + 1, 8)
    n_tok = n_exp * TOK_DEV
    n_pieces = 1 + len(V_PARTS)
    few = round_up((2 * real_cols - 1) // RANK + 2, 8)
    any_space = pl.BlockSpec(memory_space=pl.ANY)
    turned = pl.pallas_call(
        functools.partial(kernel, (*dims, units)),
        name="influence_exchange",
        out_shape=pltpu.VMEM((queries, TOK_DEV), jnp.float32),
        in_specs=[pl.BlockSpec(memory_space=pltpu.SMEM)] + [any_space] * 5,
        out_specs=pl.BlockSpec(memory_space=pltpu.VMEM),
        scratch_shapes=[
            pltpu.VMEM((1, slots), jnp.int32),
            pltpu.VMEM((slots, width), jnp.bfloat16),
            pltpu.VMEM((n_tok, width), jnp.bfloat16),
            pltpu.VMEM((n_dp, cols, width), jnp.bfloat16),
            pltpu.VMEM((2, 2, cols, n_tok), jnp.float32),
            pltpu.VMEM((2, 2, cols, n_tok), jnp.float32),
            pltpu.VMEM((depth, n_tok), jnp.float32),
            pltpu.VMEM((n_tok, slots), jnp.bfloat16),
            pltpu.VMEM((2, n_tok, LANES), jnp.float32),
            pltpu.VMEM((n_exp, depth, TOK_DEV), jnp.float32),
            pltpu.VMEM((n_exp, few, TOK_DEV), jnp.float32),
            pltpu.VMEM((n_exp, few, TOK_DEV), jnp.float32),
            pltpu.SemaphoreType.DMA((3,)),
            pltpu.SemaphoreType.DMA((1,)),
            pltpu.SemaphoreType.DMA((1,)),
            pltpu.SemaphoreType.DMA((steps, n_pieces)),
            pltpu.SemaphoreType.DMA((steps, n_pieces)),
            pltpu.SemaphoreType.DMA((2,)),
            pltpu.SemaphoreType.DMA((2,)),
        ],
        compiler_params=pltpu.CompilerParams(
            collective_id=0, has_side_effects=True, vmem_limit_bytes=60 * 1024 * 1024
        ),
    )(counts, row_token, row_acts[0], row_grads[0], gfac, vfac)
    return turned.T


def solution(mesh):
    n_exp, n_dp = mesh.shape["expert"], mesh.shape["dp"]
    across = len({d.coords[0] for d in mesh.devices.flat})

    def whole(row_acts, row_grads, grad_factor, value_factor, counts, row_token):
        all_cols = grad_factor.shape[2]
        real_cols = all_cols // n_dp
        granule = real_cols if RANK % real_cols == 0 else RANK
        while real_cols % granule:
            granule //= 2
        dims = (n_dp, n_exp, across, all_cols // RANK, real_cols, granule)
        return jax.shard_map(
            functools.partial(local, dims),
            mesh=mesh,
            in_specs=(
                P("expert", "dp", None),
                P("expert", "dp", None),
                P("expert", None, "dp"),
                P("expert", None, "dp"),
                P("expert", "dp"),
                P("expert", "dp"),
            ),
            out_specs=P(("expert", "dp"), None),
            check_vma=False,
        )(row_acts, row_grads, grad_factor, value_factor, counts, row_token)

    return whole
```

time: 32.2 us -> 31.1 us (0.966)
  Pallas kernels: 30.7 us -> 29.6 us
    pallas_call x1, Pallas kernels: 30.7 us -> 29.6 us  [local(): pl.pallas_call(functools.partial(kernel, (*dims, units)), name='influence...]
where the time goes in v2:
time: 31.1 us; the launch traced here: 30.9 us
  Pallas kernels  29.6 us (95%)
  between operations  0.66 us (2%)
  local copies, waits for them, and re-layouts  0.61 us (2%)
    pallas_call x1, Pallas kernels, local(): pl.pallas_call(functools.partial(kernel, (*dims, units)), name='influence...  29.6 us

profile of v2, /device:TPU:0, one launch (start us, length us, event | category | flops | bytes accessed | tf_op | source)
XLA Modules:
  0.0 30.9 jit_solution(17310565162698859254)
XLA Ops:
  0.7 29.6 %influence_exchange.1 = f32[24,256]{1,0:T(8,128)S(1)} custom-call(s32[1,1]{1,0:T(1,128)S(6)} %copy.9.count_ref, s32[1,1024]{1,0:T(1,128)} %token_hbm.1, bf16[1024,2048]{1,0:T(8,128)(2,1)} %bitcast.10, bf16[1024,768]{1,0:T(8,128)(2,1)} %bitcast.11, bf16[96,768]{1,0:T(8,128)(2,1)} %bitcast.13, bf16[96,2048]{1,0:T(8,128)(2,1)} %bitcast.12), custom_call_target="tpu_custom_call" | custom-call | tf_op jit(solution)/shard_map/influence_exchange/pallas_call | solution.py:374
  30.3 0.6 %copy.8 = f32[256,24]{0,1:T(8,128)} copy(f32[256,24]{0,1:T(8,128)S(1)} %bitcast.9) | data formatting | bytes 49152

commit v3 on v2

--- a/solution.py
+++ b/solution.py
@@ -11,7 +11,7 @@
 TOK_DEV = 256
 LANES = 128
 PACK = 16
-V_PARTS = (2, 4, 8, 8)
+V_EIGHTHS = (3, 2, 2, 1)
 CHUNK = 256
 CHUNKS_BEFORE_RELAY = 8
 
@@ -36,9 +36,12 @@
     tokens,
     rows,
     by_token,
+    mate,
     fac,
     gproj,
     aproj,
+    edge_g,
+    edge_a,
     scores,
     onehot,
     energies,
@@ -50,6 +53,7 @@
     own_sem,
     direct_sem,
     relay_sem,
+    mate_sem,
     zsend_sem,
     zrecv_sem,
 ):
@@ -81,9 +85,9 @@
     partner = mine * 2 + other
 
     pieces, start = [pl.ds(0, units)], units
-    for part in V_PARTS:
-        pieces.append(pl.ds(start, model // part))
-        start += model // part
+    for part in V_EIGHTHS:
+        pieces.append(pl.ds(start, part * model // 8))
+        start += part * model // 8
     n_pieces = len(pieces)
     last_piece = n_pieces - 1
 
@@ -191,18 +195,17 @@
     def of_owner(owner):
         return pl.ds(pl.multiple_of(owner * TOK_DEV, TOK_DEV), TOK_DEV)
 
-    def hand_over(stage, src, dst, owner):
+    def hand_over(stage, src, dst, owner, target=me):
         pltpu.make_async_remote_copy(
             src_ref=src,
             dst_ref=dst,
             send_sem=zsend_sem.at[stage],
             recv_sem=zrecv_sem.at[stage],
-            device_id=(owner, me),
+            device_id=(owner, target),
             device_id_type=MESH,
         ).start()
 
-    def handed(stage, ref):
-        all_of = ref.at[pl.ds(0, n_exp - 1)]
+    def handed(stage, all_of):
         return pltpu.make_async_remote_copy(
             src_ref=all_of,
             dst_ref=all_of,
@@ -240,7 +243,9 @@
         wait_for(fac.at[pl.ds(0, count), :, pieces[j]], relay_sem.at[step - 1, j])
 
     far_chip = chip_at(half)
-    base = 2 * far_chip * real_cols // RANK
+
+    def base_of(side):
+        return (2 * far_chip + side) * real_cols // RANK
 
     def multiply(step, j):
         sources = sources_of(step)
@@ -260,98 +265,178 @@
                     for query, total in group_sums(chip, side, product[buf, side]):
                         scores[pl.ds(query, 1)] += total
 
+    far_owner = owner_at(0)
+    edge_tok = of_owner(far_owner)
+    rest = pl.ds(
+        pl.multiple_of(jnp.where(far_owner == 0, TOK_DEV, 0), TOK_DEV), n_tok - TOK_DEV
+    )
+
+    def lend(part, span):
+        pltpu.make_async_remote_copy(
+            src_ref=by_token.at[edge_tok, span],
+            dst_ref=mate.at[:, span],
+            send_sem=mate_sem.at[2],
+            recv_sem=mate_sem.at[part],
+            device_id=(me_e, partner),
+            device_id_type=MESH,
+        ).start()
+
     with jax.named_scope("perm"):
-        for chunk in chunks[:CHUNKS_BEFORE_RELAY]:
+        for at, chunk in enumerate(chunks):
             order_rows(*chunk)
-    with jax.named_scope("pass10"):
-        pass_on(1, 0)
-    with jax.named_scope("perm2"):
-        for chunk in chunks[CHUNKS_BEFORE_RELAY:]:
-            order_rows(*chunk)
+            if chunk[0] == units:
+                lend(0, g_span)
+            if at == CHUNKS_BEFORE_RELAY - 1:
+                with jax.named_scope("pass10"):
+                    pass_on(1, 0)
     with jax.named_scope("energy"):
         totals = [
             jnp.sum(energies[kind].T, axis=0, keepdims=True) for kind in range(2)
         ]
         scores[queries : queries + 1] = totals[0] * totals[1]
-
-    with jax.named_scope("mine"):
+    lend(1, v_span)
+
+    with jax.named_scope("mineg"):
         own_shard = fac.at[own_slot]
         pltpu.make_async_copy(own_shard, own_shard, load_sem.at[2]).wait()
         wait_for(own_shard, own_sem.at[0])
-        product = project_pair([mine], v_span)[0] * project_pair([mine], g_span)[0]
+        gproj[0] = project_pair([mine], g_span)[0]
+    with jax.named_scope("pass11"):
+        pass_on(1, 1)
+    with jax.named_scope("minev"):
+        product = project_pair([mine], v_span)[0] * gproj[0]
         for side in range(2):
             for query, total in group_sums(mine, side, product[side]):
                 scores[pl.ds(query, 1)] += total
 
-    order = [(step, j) for step in range(1, half + 1) for j in range(n_pieces)]
+    def edge_products(j):
+        factor = fac[2 * far_chip + core, :, pieces[j]]
+        return [
+            project(factor, by_token.at[edge_tok], pieces[j]),
+            project(factor, mate, pieces[j]),
+        ]
+
+    def edge_multiply(j):
+        if j < 2:
+            wait_for(mate.at[:, (g_span, v_span)[j]], mate_sem.at[j])
+        for kind, value in enumerate(edge_products(j)):
+            if j == 0:
+                edge_g[kind] = value
+            elif j == 1:
+                edge_a[kind] = value
+            else:
+                edge_a[kind] += value
+
+    def rest_multiply(j):
+        relayed(half, j)
+        factor = fac[pl.ds(2 * far_chip, 2), :, pieces[j]]
+        factor = factor.reshape(2 * cols, pieces[j].size)
+        value = project(factor, by_token.at[rest], pieces[j])
+        value = value.reshape(2, cols, n_tok - TOK_DEV)
+        if j == 0:
+            gproj[0, :, :, rest] = value
+        elif j == 1:
+            aproj[0, :, :, rest] = value
+        else:
+            aproj[0, :, :, rest] += value
+
+    order = [(step, j) for step in range(1, half) for j in range(n_pieces)]
     for at, event in enumerate(order):
-        if not at:
-            continue
-        with jax.named_scope(f"pass{event[0]}{event[1]}"):
-            pass_on(*event)
-        with jax.named_scope(f"mul{order[at - 1][0]}{order[at - 1][1]}"):
-            multiply(*order[at - 1])
-        if event == (half, 0):
-            with jax.named_scope("near"):
-                for k in range(n_exp - 1):
-                    owner = owner_at(k)
-                    hand_over(0, scores.at[:, of_owner(owner)], landed.at[me_e], owner)
-
-    def far_sums(side, owner, product):
+        if at > 1:
+            with jax.named_scope(f"pass{event[0]}{event[1]}"):
+                pass_on(*event)
+        if at:
+            with jax.named_scope(f"mul{order[at - 1][0]}{order[at - 1][1]}"):
+                multiply(*order[at - 1])
+    with jax.named_scope("mullast"):
+        multiply(*order[-1])
+    with jax.named_scope("near"):
+        for k in range(n_exp - 1):
+            owner = owner_at(k)
+            hand_over(0, scores.at[:, of_owner(owner)], landed.at[me_e], owner)
+    for j in range(last_piece):
+        with jax.named_scope(f"pass{half}{j}"):
+            pass_on(half, j)
+        with jax.named_scope(f"edge{j}"):
+            edge_multiply(j)
+        if j:
+            with jax.named_scope(f"rest{j - 1}"):
+                rest_multiply(j - 1)
+    with jax.named_scope(f"pass{half}{last_piece}"):
+        pass_on(half, last_piece)
+
+    def far_sums(owner, side, product):
         for query, total in group_sums(far_chip, side, product):
-            far_dense[owner, pl.ds(query - base, 1)] += total
-
-    span = pieces[last_piece]
-    with jax.named_scope("ownhalf"):
-        value = project(fac[2 * far_chip + core, :, span], by_token, span)
-        product = (aproj[0, core] + value) * gproj[0, core]
-        for owner in range(n_exp):
-            far_sums(core, owner, product[:, owner * TOK_DEV : (owner + 1) * TOK_DEV])
+            far_dense[owner, side, query - base_of(side)] += total
+
+    with jax.named_scope("edge"):
+        for kind, value in enumerate(edge_products(last_piece)):
+            product = (edge_a[kind] + value) * edge_g[kind]
+            for query, total in group_sums(far_chip, core, product):
+                far_dense[far_owner, kind, query - base_of(core)] += total
+            hand_over(
+                1,
+                far_dense.at[far_owner, kind],
+                far_landed.at[me_e, core],
+                far_owner,
+                partner if kind else me,
+            )
+    with jax.named_scope("restprev"):
+        rest_multiply(last_piece - 1)
     with jax.named_scope("lastrelay"):
         relayed(half, last_piece)
     with jax.named_scope("far"):
-        for k in range(n_exp):
+        span = pieces[last_piece]
+        factor = fac[pl.ds(2 * far_chip, 2), :, span].reshape(2 * cols, span.size)
+        for k in range(1, n_exp):
             owner = owner_at(k) if k < n_exp - 1 else me_e
             tok = of_owner(owner)
-            value = lax.dot_general(
-                fac[2 * far_chip + other, :, span],
-                by_token[tok, span],
-                CONTRACT_LAST,
-                preferred_element_type=jnp.float32,
-            )
-            far_sums(other, owner, (aproj[0, other, :, tok] + value) * gproj[0, other, :, tok])
+            value = project(factor, by_token.at[tok], span).reshape(2, cols, TOK_DEV)
+            for side in range(2):
+                far_sums(
+                    owner,
+                    side,
+                    (aproj[0, side, :, tok] + value[side]) * gproj[0, side, :, tok],
+                )
             if k < n_exp - 1:
                 hand_over(1, far_dense.at[owner], far_landed.at[me_e], owner)
 
-    near_wait, far_wait = handed(0, landed), handed(1, far_landed)
     with jax.named_scope("colnear"):
         result = scores[:, of_owner(me_e)]
+        near_wait = handed(0, landed.at[pl.ds(0, n_exp - 1)])
         near_wait.wait_recv()
         for k in range(n_exp - 1):
             result = result + landed[owner_at(k)]
         factor = lax.rsqrt(result[queries : queries + 1] / (model * units) + epsilon)
         factor = factor / jnp.sqrt(jnp.float32(RANK))
-        late = far_dense[me_e]
     with jax.named_scope("colfar"):
+        far_wait = handed(1, far_landed.at[pl.ds(0, n_exp - 1)])
         far_wait.wait_recv()
+    late = far_dense[me_e]
     for k in range(n_exp - 1):
         late = late + far_landed[owner_at(k)]
     row_ids = lax.broadcasted_iota(jnp.int32, result.shape, 0)
-    for i in range(late.shape[0]):
-        result = result + jnp.where(row_ids == base + i, late[i : i + 1], 0.0)
+    for side in range(2):
+        for i in range(late.shape[1]):
+            row = row_ids == base_of(side) + i
+            result = result + jnp.where(row, late[side, i], 0.0)
     out_ref[...] = result[:queries] * factor
     with jax.named_scope("sends"):
         near_wait.wait_send()
         far_wait.wait_send()
-        all_sent = fac.at[pl.ds(0, sum(sent) // (cols * width))]
-        pltpu.make_async_remote_copy(
-            src_ref=all_sent,
-            dst_ref=all_sent,
-            send_sem=send_sem.at[0],
-            recv_sem=own_sem.at[0],
-            device_id=(me_e, partner),
-            device_id_type=MESH,
-        ).wait_send()
+
+        def sent_all(ref, sem):
+            pltpu.make_async_remote_copy(
+                src_ref=ref,
+                dst_ref=ref,
+                send_sem=sem,
+                recv_sem=own_sem.at[0],
+                device_id=(me_e, partner),
+                device_id_type=MESH,
+            ).wait_send()
+
+        sent_all(mate, mate_sem.at[2])
+        sent_all(fac.at[pl.ds(0, sum(sent) // (cols * width))], send_sem.at[0])
 
 
 def local(dims, row_acts, row_grads, grad_factor, value_factor, counts, row_token):
@@ -368,8 +453,8 @@
     steps = chips // 2
     depth = round_up(queries + 1, 8)
     n_tok = n_exp * TOK_DEV
-    n_pieces = 1 + len(V_PARTS)
-    few = round_up((2 * real_cols - 1) // RANK + 2, 8)
+    n_pieces = 1 + len(V_EIGHTHS)
+    few = real_cols // RANK if real_cols % RANK == 0 else (real_cols - 1) // RANK + 2
     any_space = pl.BlockSpec(memory_space=pl.ANY)
     turned = pl.pallas_call(
         functools.partial(kernel, (*dims, units)),
@@ -381,20 +466,24 @@
             pltpu.VMEM((1, slots), jnp.int32),
             pltpu.VMEM((slots, width), jnp.bfloat16),
             pltpu.VMEM((n_tok, width), jnp.bfloat16),
+            pltpu.VMEM((TOK_DEV, width), jnp.bfloat16),
             pltpu.VMEM((n_dp, cols, width), jnp.bfloat16),
             pltpu.VMEM((2, 2, cols, n_tok), jnp.float32),
             pltpu.VMEM((2, 2, cols, n_tok), jnp.float32),
+            pltpu.VMEM((2, cols, TOK_DEV), jnp.float32),
+            pltpu.VMEM((2, cols, TOK_DEV), jnp.float32),
             pltpu.VMEM((depth, n_tok), jnp.float32),
             pltpu.VMEM((n_tok, slots), jnp.bfloat16),
             pltpu.VMEM((2, n_tok, LANES), jnp.float32),
             pltpu.VMEM((n_exp, depth, TOK_DEV), jnp.float32),
-            pltpu.VMEM((n_exp, few, TOK_DEV), jnp.float32),
-            pltpu.VMEM((n_exp, few, TOK_DEV), jnp.float32),
+            pltpu.VMEM((n_exp, 2, few, 1, TOK_DEV), jnp.float32),
+            pltpu.VMEM((n_exp, 2, few, 1, TOK_DEV), jnp.float32),
             pltpu.SemaphoreType.DMA((3,)),
             pltpu.SemaphoreType.DMA((1,)),
             pltpu.SemaphoreType.DMA((1,)),
             pltpu.SemaphoreType.DMA((steps, n_pieces)),
             pltpu.SemaphoreType.DMA((steps, n_pieces)),
+            pltpu.SemaphoreType.DMA((3,)),
             pltpu.SemaphoreType.DMA((2,)),
             pltpu.SemaphoreType.DMA((2,)),
         ],

time: 31.1 us -> 30.1 us (0.968)
  Pallas kernels: 29.6 us -> 28.7 us
    pallas_call x1, Pallas kernels: 29.6 us -> 28.7 us  [local(): pl.pallas_call(functools.partial(kernel, (*dims, units)), name='influence...]
where the time goes in v3:
time: 30.1 us; the launch traced here: 29.9 us
  Pallas kernels  28.7 us (95%)
  between operations  0.66 us (2%)
  local copies, waits for them, and re-layouts  0.61 us (2%)
    pallas_call x1, Pallas kernels, local(): pl.pallas_call(functools.partial(kernel, (*dims, units)), name='influence...  28.7 us
    unnamed x1, local copies, waits for them, and re-layouts  0.61 us

profile of v3, /device:TPU:0, one launch (start us, length us, event | category | flops | bytes accessed | tf_op | source)
XLA Modules:
  0.0 29.9 jit_solution(2598111697013377861)
XLA Ops:
  0.7 28.7 %influence_exchange.1 = f32[24,256]{1,0:T(8,128)S(1)} custom-call(s32[1,1]{1,0:T(1,128)S(6)} %copy.9.count_ref, s32[1,1024]{1,0:T(1,128)} %token_hbm.1, bf16[1024,2048]{1,0:T(8,128)(2,1)} %bitcast.10, bf16[1024,768]{1,0:T(8,128)(2,1)} %bitcast.11, bf16[96,768]{1,0:T(8,128)(2,1)} %bitcast.13, bf16[96,2048]{1,0:T(8,128)(2,1)} %bitcast.12), custom_call_target="tpu_custom_call" | custom-call | tf_op jit(solution)/shard_map/influence_exchange/pallas_call | solution.py:459
  29.3 0.6 %copy.8 = f32[256,24]{0,1:T(8,128)} copy(f32[256,24]{0,1:T(8,128)S(1)} %bitcast.9) | data formatting | bytes 49152

commit v4 on v3

--- a/solution.py
+++ b/solution.py
@@ -265,17 +265,22 @@
                     for query, total in group_sums(chip, side, product[buf, side]):
                         scores[pl.ds(query, 1)] += total
 
-    far_owner = owner_at(0)
-    edge_tok = of_owner(far_owner)
-    rest = pl.ds(
-        pl.multiple_of(jnp.where(far_owner == 0, TOK_DEV, 0), TOK_DEV), n_tok - TOK_DEV
-    )
-
-    def lend(part, span):
+    edge = mate.shape[0]
+    lower = 2 * me_e < n_exp
+    edge_start = pl.multiple_of(jnp.where(lower, n_tok - edge, 0), TOK_DEV)
+    rest_start = pl.multiple_of(jnp.where(lower, 0, edge), TOK_DEV)
+    edge_tok, rest = pl.ds(edge_start, edge), pl.ds(rest_start, n_tok - edge)
+    middle = pieces[3].start
+    mate_spans = [
+        g_span, pl.ds(units, middle - units), pl.ds(middle, width - middle)
+    ]
+
+    def lend(part):
+        span = mate_spans[part]
         pltpu.make_async_remote_copy(
             src_ref=by_token.at[edge_tok, span],
             dst_ref=mate.at[:, span],
-            send_sem=mate_sem.at[2],
+            send_sem=mate_sem.at[3],
             recv_sem=mate_sem.at[part],
             device_id=(me_e, partner),
             device_id_type=MESH,
@@ -284,8 +289,9 @@
     with jax.named_scope("perm"):
         for at, chunk in enumerate(chunks):
             order_rows(*chunk)
-            if chunk[0] == units:
-                lend(0, g_span)
+            for part in range(2):
+                if chunk[0] == mate_spans[part + 1].start:
+                    lend(part)
             if at == CHUNKS_BEFORE_RELAY - 1:
                 with jax.named_scope("pass10"):
                     pass_on(1, 0)
@@ -294,7 +300,7 @@
             jnp.sum(energies[kind].T, axis=0, keepdims=True) for kind in range(2)
         ]
         scores[queries : queries + 1] = totals[0] * totals[1]
-    lend(1, v_span)
+    lend(2)
 
     with jax.named_scope("mineg"):
         own_shard = fac.at[own_slot]
@@ -309,30 +315,35 @@
             for query, total in group_sums(mine, side, product[side]):
                 scores[pl.ds(query, 1)] += total
 
-    def edge_products(j):
+    def edge_product(j):
+        for part, span in enumerate(mate_spans):
+            if pieces[j].start == span.start:
+                wait_for(mate.at[:, span], mate_sem.at[part])
         factor = fac[2 * far_chip + core, :, pieces[j]]
-        return [
-            project(factor, by_token.at[edge_tok], pieces[j]),
-            project(factor, mate, pieces[j]),
-        ]
+        both = jnp.concatenate([by_token[edge_tok, pieces[j]], mate[:, pieces[j]]], axis=0)
+        value = lax.dot_general(
+            factor, both, CONTRACT_LAST, preferred_element_type=jnp.float32
+        )
+        return [value[:, :edge], value[:, edge:]]
 
     def edge_multiply(j):
-        if j < 2:
-            wait_for(mate.at[:, (g_span, v_span)[j]], mate_sem.at[j])
-        for kind, value in enumerate(edge_products(j)):
+        for kind, part in enumerate(edge_product(j)):
             if j == 0:
-                edge_g[kind] = value
+                edge_g[kind] = part
             elif j == 1:
-                edge_a[kind] = value
+                edge_a[kind] = part
             else:
-                edge_a[kind] += value
-
-    def rest_multiply(j):
-        relayed(half, j)
+                edge_a[kind] += part
+
+    def rest_product(j):
         factor = fac[pl.ds(2 * far_chip, 2), :, pieces[j]]
         factor = factor.reshape(2 * cols, pieces[j].size)
         value = project(factor, by_token.at[rest], pieces[j])
-        value = value.reshape(2, cols, n_tok - TOK_DEV)
+        return value.reshape(2, cols, n_tok - edge)
+
+    def rest_multiply(j):
+        relayed(half, j)
+        value = rest_product(j)
         if j == 0:
             gproj[0, :, :, rest] = value
         elif j == 1:
@@ -359,47 +370,47 @@
             pass_on(half, j)
         with jax.named_scope(f"edge{j}"):
             edge_multiply(j)
-        if j:
-            with jax.named_scope(f"rest{j - 1}"):
-                rest_multiply(j - 1)
+        if j > 1:
+            with jax.named_scope(f"rest{j - 2}"):
+                rest_multiply(j - 2)
     with jax.named_scope(f"pass{half}{last_piece}"):
         pass_on(half, last_piece)
 
-    def far_sums(owner, side, product):
+    def far_sums(kind, side, product, first, count):
         for query, total in group_sums(far_chip, side, product):
-            far_dense[owner, side, query - base_of(side)] += total
-
+            for i in range(count):
+                far_dense[first + i, kind, query - base_of(side)] += total[
+                    :, i * TOK_DEV : (i + 1) * TOK_DEV
+                ]
+
+    n_edge = edge // TOK_DEV
+    edge_first = jnp.where(lower, n_exp - n_edge, 0)
+    rest_first = jnp.where(lower, 0, n_edge)
     with jax.named_scope("edge"):
-        for kind, value in enumerate(edge_products(last_piece)):
+        for kind, value in enumerate(edge_product(last_piece)):
             product = (edge_a[kind] + value) * edge_g[kind]
-            for query, total in group_sums(far_chip, core, product):
-                far_dense[far_owner, kind, query - base_of(core)] += total
-            hand_over(
-                1,
-                far_dense.at[far_owner, kind],
-                far_landed.at[me_e, core],
-                far_owner,
-                partner if kind else me,
-            )
-    with jax.named_scope("restprev"):
-        rest_multiply(last_piece - 1)
+            far_sums(kind, core, product, edge_first, n_edge)
+            for k in range(n_edge):
+                hand_over(
+                    1,
+                    far_dense.at[owner_at(k), kind],
+                    far_landed.at[me_e, core],
+                    owner_at(k),
+                    partner if kind else me,
+                )
+    for j in range(max(last_piece - 2, 0), last_piece):
+        with jax.named_scope(f"rest{j}"):
+            rest_multiply(j)
     with jax.named_scope("lastrelay"):
         relayed(half, last_piece)
     with jax.named_scope("far"):
-        span = pieces[last_piece]
-        factor = fac[pl.ds(2 * far_chip, 2), :, span].reshape(2 * cols, span.size)
-        for k in range(1, n_exp):
-            owner = owner_at(k) if k < n_exp - 1 else me_e
-            tok = of_owner(owner)
-            value = project(factor, by_token.at[tok], span).reshape(2, cols, TOK_DEV)
-            for side in range(2):
-                far_sums(
-                    owner,
-                    side,
-                    (aproj[0, side, :, tok] + value[side]) * gproj[0, side, :, tok],
-                )
-            if k < n_exp - 1:
-                hand_over(1, far_dense.at[owner], far_landed.at[me_e], owner)
+        value = rest_product(last_piece)
+        for side in range(2):
+            product = (aproj[0, side, :, rest] + value[side]) * gproj[0, side, :, rest]
+            far_sums(side, side, product, rest_first, n_exp - n_edge)
+        for k in range(n_edge, n_exp - 1):
+            owner = owner_at(k)
+            hand_over(1, far_dense.at[owner], far_landed.at[me_e], owner)
 
     with jax.named_scope("colnear"):
         result = scores[:, of_owner(me_e)]
@@ -435,7 +446,7 @@
                 device_id_type=MESH,
             ).wait_send()
 
-        sent_all(mate, mate_sem.at[2])
+        sent_all(mate, mate_sem.at[3])
         sent_all(fac.at[pl.ds(0, sum(sent) // (cols * width))], send_sem.at[0])
 
 
@@ -453,6 +464,7 @@
     steps = chips // 2
     depth = round_up(queries + 1, 8)
     n_tok = n_exp * TOK_DEV
+    edge = n_exp // 2 * TOK_DEV
     n_pieces = 1 + len(V_EIGHTHS)
     few = real_cols // RANK if real_cols % RANK == 0 else (real_cols - 1) // RANK + 2
     any_space = pl.BlockSpec(memory_space=pl.ANY)
@@ -466,12 +478,12 @@
             pltpu.VMEM((1, slots), jnp.int32),
             pltpu.VMEM((slots, width), jnp.bfloat16),
             pltpu.VMEM((n_tok, width), jnp.bfloat16),
-            pltpu.VMEM((TOK_DEV, width), jnp.bfloat16),
+            pltpu.VMEM((edge, width), jnp.bfloat16),
             pltpu.VMEM((n_dp, cols, width), jnp.bfloat16),
             pltpu.VMEM((2, 2, cols, n_tok), jnp.float32),
             pltpu.VMEM((2, 2, cols, n_tok), jnp.float32),
-            pltpu.VMEM((2, cols, TOK_DEV), jnp.float32),
-            pltpu.VMEM((2, cols, TOK_DEV), jnp.float32),
+            pltpu.VMEM((2, cols, edge), jnp.float32),
+            pltpu.VMEM((2, cols, edge), jnp.float32),
             pltpu.VMEM((depth, n_tok), jnp.float32),
             pltpu.VMEM((n_tok, slots), jnp.bfloat16),
             pltpu.VMEM((2, n_tok, LANES), jnp.float32),
@@ -483,7 +495,7 @@
             pltpu.SemaphoreType.DMA((1,)),
             pltpu.SemaphoreType.DMA((steps, n_pieces)),
             pltpu.SemaphoreType.DMA((steps, n_pieces)),
-            pltpu.SemaphoreType.DMA((3,)),
+            pltpu.SemaphoreType.DMA((4,)),
             pltpu.SemaphoreType.DMA((2,)),
             pltpu.SemaphoreType.DMA((2,)),
         ],

time: 30.1 us -> 29.8 us (0.990)
  no operation moved by 1% of the time
where the time goes in v4:
time: 29.8 us; the launch traced here: 29.7 us
  Pallas kernels  28.4 us (95%)
  between operations  0.66 us (2%)
  local copies, waits for them, and re-layouts  0.61 us (2%)
    pallas_call x1, Pallas kernels, local(): pl.pallas_call(functools.partial(kernel, (*dims, units)), name='influence...  28.4 us
    unnamed x1, local copies, waits for them, and re-layouts  0.61 us

profile of v4, /device:TPU:0, one launch (start us, length us, event | category | flops | bytes accessed | tf_op | source)
XLA Modules:
  0.0 29.7 jit_solution(17965180543580117887)
XLA Ops:
  0.7 28.4 %influence_exchange.1 = f32[24,256]{1,0:T(8,128)S(1)} custom-call(s32[1,1]{1,0:T(1,128)S(6)} %copy.9.count_ref, s32[1,1024]{1,0:T(1,128)} %token_hbm.1, bf16[1024,2048]{1,0:T(8,128)(2,1)} %bitcast.10, bf16[1024,768]{1,0:T(8,128)(2,1)} %bitcast.11, bf16[96,768]{1,0:T(8,128)(2,1)} %bitcast.13, bf16[96,2048]{1,0:T(8,128)(2,1)} %bitcast.12), custom_call_target="tpu_custom_call" | custom-call | tf_op jit(solution)/shard_map/influence_exchange/pallas_call | solution.py:471
  29.1 0.6 %copy.8 = f32[256,24]{0,1:T(8,128)} copy(f32[256,24]{0,1:T(8,128)S(1)} %bitcast.9) | data formatting | bytes 49152

commit v5 on v4

--- a/solution.py
+++ b/solution.py
@@ -132,18 +132,20 @@
     own_slot = mine * 2 + core
     load_tokens = pltpu.make_async_copy(token_hbm, tokens, load_sem.at[0])
     load_tokens.start()
+    pltpu.make_async_copy(gfac_hbm, fac.at[own_slot, :, g_span], load_sem.at[2]).start()
+    pltpu.make_async_copy(vfac_hbm, fac.at[own_slot, :, v_span], load_sem.at[2]).start()
     pltpu.make_async_copy(grads_hbm, rows.at[:, g_span], load_sem.at[1]).start()
     pltpu.make_async_copy(acts_hbm, rows.at[:, v_span], load_sem.at[1]).start()
-    pltpu.make_async_copy(gfac_hbm, fac.at[own_slot, :, g_span], load_sem.at[2]).start()
-    pltpu.make_async_copy(vfac_hbm, fac.at[own_slot, :, v_span], load_sem.at[2]).start()
     with jax.named_scope("barrier"):
         pl.semaphore_wait(barrier, 3 + n_exp - 1)
 
+    own_shard = fac.at[own_slot]
+    pltpu.make_async_copy(own_shard, own_shard, load_sem.at[2]).wait()
     for j in range(n_pieces):
         for target in (ahead, behind):
-            send(own(j), fac.at[own_slot, :, pieces[j]], direct_sem.at[0, j], target)
-    send(gfac_hbm, fac.at[own_slot, :, g_span], own_sem.at[0], partner)
-    send(vfac_hbm, fac.at[own_slot, :, v_span], own_sem.at[0], partner)
+            part = fac.at[own_slot, :, pieces[j]]
+            send(part, part, direct_sem.at[0, j], target)
+    send(own_shard, own_shard, own_sem.at[0], partner)
 
     with jax.named_scope("onehot"):
         load_tokens.wait()
@@ -304,7 +306,6 @@
 
     with jax.named_scope("mineg"):
         own_shard = fac.at[own_slot]
-        pltpu.make_async_copy(own_shard, own_shard, load_sem.at[2]).wait()
         wait_for(own_shard, own_sem.at[0])
         gproj[0] = project_pair([mine], g_span)[0]
     with jax.named_scope("pass11"):

time: 29.8 us -> 29.6 us (level)
  no operation moved by 1% of the time
where the time goes in v5:
time: 29.6 us; the launch traced here: 29.4 us
  Pallas kernels  28.2 us (95%)
  between operations  0.66 us (2%)
  local copies, waits for them, and re-layouts  0.61 us (2%)
    pallas_call x1, Pallas kernels, local(): pl.pallas_call(functools.partial(kernel, (*dims, units)), name='influence...  28.2 us
    unnamed x1, local copies, waits for them, and re-layouts  0.61 us

profile of v5, /device:TPU:0, one launch (start us, length us, event | category | flops | bytes accessed | tf_op | source)
XLA Modules:
  0.0 29.4 jit_solution(10156181168978170020)
XLA Ops:
  0.7 28.2 %influence_exchange.1 = f32[24,256]{1,0:T(8,128)S(1)} custom-call(s32[1,1]{1,0:T(1,128)S(6)} %copy.9.count_ref, s32[1,1024]{1,0:T(1,128)} %token_hbm.1, bf16[1024,2048]{1,0:T(8,128)(2,1)} %bitcast.10, bf16[1024,768]{1,0:T(8,128)(2,1)} %bitcast.11, bf16[96,768]{1,0:T(8,128)(2,1)} %bitcast.13, bf16[96,2048]{1,0:T(8,128)(2,1)} %bitcast.12), custom_call_target="tpu_custom_call" | custom-call | tf_op jit(solution)/shard_map/influence_exchange/pallas_call | solution.py:472
  28.8 0.6 %copy.8 = f32[256,24]{0,1:T(8,128)} copy(f32[256,24]{0,1:T(8,128)S(1)} %bitcast.9) | data formatting | bytes 49152

commit v6 on v5

--- a/solution.py
+++ b/solution.py
@@ -90,6 +90,12 @@
         start += part * model // 8
     n_pieces = len(pieces)
     last_piece = n_pieces - 1
+    joined = pl.ds(pieces[-2].start, pieces[-2].size + pieces[-1].size)
+    coarse = pieces[:-2] + [joined]
+
+    def piece_of(step, j):
+        return pieces[j] if step == half else coarse[j]
+
 
     def own(j):
         if j == 0:
@@ -141,9 +147,9 @@
 
     own_shard = fac.at[own_slot]
     pltpu.make_async_copy(own_shard, own_shard, load_sem.at[2]).wait()
-    for j in range(n_pieces):
+    for j in range(len(coarse)):
         for target in (ahead, behind):
-            part = fac.at[own_slot, :, pieces[j]]
+            part = fac.at[own_slot, :, coarse[j]]
             send(part, part, direct_sem.at[0, j], target)
     send(own_shard, own_shard, own_sem.at[0], partner)
 
@@ -223,10 +229,10 @@
     def pass_on(step, j):
         sources = sources_of(step)
         count = len(sources)
-        span = pieces[j]
+        span = piece_of(step, j)
         wait_for(fac.at[pl.ds(0, count), :, span], direct_sem.at[step - 1, j])
 
-        def relay(chip, sem, target):
+        def relay(chip, sem, target, span=span):
             part = fac.at[2 * chip + core, :, span]
             send(part, part, sem, target)
 
@@ -236,13 +242,14 @@
         elif step == half - 1:
             chip = chip_at(step * (2 * core - 1))
             target = chip_at(1 - 2 * core) * 2 + core
-            relay(chip, direct_sem.at[step, j], target)
+            for i in range(j, n_pieces if j == len(coarse) - 1 else j + 1):
+                relay(chip, direct_sem.at[step, i], target, pieces[i])
         for chip in sources:
             relay(chip, relay_sem.at[step - 1, j], partner)
 
     def relayed(step, j):
         count = len(sources_of(step))
-        wait_for(fac.at[pl.ds(0, count), :, pieces[j]], relay_sem.at[step - 1, j])
+        wait_for(fac.at[pl.ds(0, count), :, piece_of(step, j)], relay_sem.at[step - 1, j])
 
     far_chip = chip_at(half)
 
@@ -253,12 +260,12 @@
         sources = sources_of(step)
         count = len(sources)
         relayed(step, j)
-        value = project_pair(sources, pieces[j])
+        value = project_pair(sources, piece_of(step, j))
         if j == 0:
             gproj[:count] = value
         elif j == 1:
             aproj[:count] = value
-        elif j < last_piece:
+        elif j < len(coarse) - 1:
             aproj[:count] += value
         else:
             product = (aproj[:count] + value) * gproj[:count]
@@ -352,7 +359,7 @@
         else:
             aproj[0, :, :, rest] += value
 
-    order = [(step, j) for step in range(1, half) for j in range(n_pieces)]
+    order = [(step, j) for step in range(1, half) for j in range(len(coarse))]
     for at, event in enumerate(order):
         if at > 1:
             with jax.named_scope(f"pass{event[0]}{event[1]}"):
@@ -371,7 +378,7 @@
             pass_on(half, j)
         with jax.named_scope(f"edge{j}"):
             edge_multiply(j)
-        if j > 1:
+        if 1 < j < last_piece - 1:
             with jax.named_scope(f"rest{j - 2}"):
                 rest_multiply(j - 2)
     with jax.named_scope(f"pass{half}{last_piece}"):
@@ -399,7 +406,7 @@
                     owner_at(k),
                     partner if kind else me,
                 )
-    for j in range(max(last_piece - 2, 0), last_piece):
+    for j in range(last_piece - 3, last_piece):
         with jax.named_scope(f"rest{j}"):
             rest_multiply(j)
     with jax.named_scope("lastrelay"):

time: 29.6 us -> 29.7 us (level)
  no operation moved by 1% of the time
where the time goes in v6:
time: 29.7 us; the launch traced here: 29.5 us
  Pallas kernels  28.2 us (95%)
  between operations  0.66 us (2%)
  local copies, waits for them, and re-layouts  0.61 us (2%)
    pallas_call x1, Pallas kernels, local(): pl.pallas_call(functools.partial(kernel, (*dims, units)), name='influence...  28.2 us
    unnamed x1, local copies, waits for them, and re-layouts  0.61 us

profile of v6, /device:TPU:0, one launch (start us, length us, event | category | flops | bytes accessed | tf_op | source)
XLA Modules:
  0.0 29.5 jit_solution(3768467527619972047)
XLA Ops:
  0.7 28.2 %influence_exchange.1 = f32[24,256]{1,0:T(8,128)S(1)} custom-call(s32[1,1]{1,0:T(1,128)S(6)} %copy.9.count_ref, s32[1,1024]{1,0:T(1,128)} %token_hbm.1, bf16[1024,2048]{1,0:T(8,128)(2,1)} %bitcast.10, bf16[1024,768]{1,0:T(8,128)(2,1)} %bitcast.11, bf16[96,768]{1,0:T(8,128)(2,1)} %bitcast.13, bf16[96,2048]{1,0:T(8,128)(2,1)} %bitcast.12), custom_call_target="tpu_custom_call" | custom-call | tf_op jit(solution)/shard_map/influence_exchange/pallas_call | solution.py:479
  28.9 0.6 %copy.8 = f32[256,24]{0,1:T(8,128)} copy(f32[256,24]{0,1:T(8,128)S(1)} %bitcast.9) | data formatting | bytes 49152
